TPU v7x, 256 devices: a whole 4x4x8 slice. The times are simulated.
256 devices in a mesh: cable: 32 (over y_lo, z, core), grid: 8 (over x, y_hi).
Axes of the slice: x: 4, y: 4 (y_hi: 2, y_lo: 2; y = y_hi * 2 + y_lo), z: 8, core: 2. Of those that a mesh axis runs over, the one named last changes fastest.
Arguments:
- green: bfloat16 [2, 8192, 16384], P(None, 'cable', 'grid'), may hold values from -6 to 6
- source_weight: float32 [16384], P('grid'), may hold values from 0.25 to 4
- observed: float32 [2, 2, 8192, 256], P(None, None, 'cable'), may hold values from -6 to 6
- amp_weight: float32 [2, 8192, 256], P(None, 'cable'), may hold values from 0.25 to 2
- pair_used: int32 [32, 2], P('cable'), may hold values 0 or 1
Outputs:
- adjoint: float32 [2, 8192, 16384], P(None, 'cable', 'grid')
- kernel: float32 [16384], P('grid')
All inputs are finite; a program needn't handle non-finite values. No bound on the sum of `pair_used` on one device may be relied on, other than what follows from the above.
Results may differ from a plain program's by a relative error of at most 0.0037.
Values may be sent and summed in bfloat16 or wider, within the bound.
No kernel may reach another device: no remote copies, remote signals or barrier semaphores. Data moves between devices by JAX's collectives and lax.ppermute only.
A program may use at most 64 MiB of HBM per device.

v0:
```python
import math
import jax
import jax.numpy as jnp
from jax import lax
from jax.sharding import PartitionSpec as P


def shifted(block, axis, distance):
    devices = range(lax.axis_size(axis))
    route = [((i - distance) % len(devices), i) for i in devices]
    return lax.ppermute(block, axis, route)


def build_block(pair_resid):
    resid_real = pair_resid[0]
    resid_imag = pair_resid[1]
    upper_half = jnp.concatenate([resid_real, resid_imag], axis=1)
    lower_half = jnp.concatenate([-resid_imag, resid_real], axis=1)
    return jnp.concatenate([upper_half, lower_half], axis=0)


def residuals(corr, observed_rows, weight_rows, pair_used):
    mask_values = pair_used[0].astype(jnp.float32)
    scaled = mask_values[:, None, None, None] * weight_rows[:, None, :, :] * (corr - observed_rows)
    return scaled.astype(jnp.bfloat16)


def shards(green, source_weight, observed, amp_weight, pair_used):
    row_count = green.shape[1]
    col_count = green.shape[2]
    block_count = lax.axis_size("cable")
    grid_count = lax.axis_size("grid")
    inv_norm = 1.0 / math.sqrt(col_count * grid_count)
    kernel_scale = inv_norm / (2.0 * math.sqrt(2.0 * block_count))
    own_block = green.reshape(2 * row_count, col_count)
    near_blocks = []
    for offset in range(2):
        near_blocks.append(shifted(own_block, "cable", offset + 1))
    weighted = (own_block.astype(jnp.float32) * source_weight[None, :]).astype(jnp.bfloat16)
    partial_list = []
    for offset in range(2):
        products = lax.dot_general(
            weighted,
            near_blocks[offset],
            (((1,), (1,)), ((), ())),
            preferred_element_type=jnp.float32,
        )
        corr_real = products[:row_count, :row_count] + products[row_count:, row_count:]
        corr_imag = products[:row_count, row_count:] - products[row_count:, :row_count]
        partial_list.append(jnp.stack([corr_real, corr_imag]))
    partials = jnp.stack(partial_list)
    summed = lax.psum(partials, "grid")
    resid = residuals(inv_norm * summed, observed, amp_weight, pair_used)
    own_float = own_block.astype(jnp.float32)
    fields = jnp.zeros((2 * row_count, col_count), jnp.float32)
    kernel_part = jnp.zeros((col_count,), jnp.float32)
    for offset in range(2):
        resid_block = build_block(resid[offset])
        later_term = jnp.dot(resid_block, near_blocks[offset], preferred_element_type=jnp.float32)
        kernel_part = kernel_part + jnp.sum(own_float * later_term, axis=0)
        fields = fields + later_term
    for offset in range(2):
        resid_block = build_block(resid[offset])
        early_term = lax.dot_general(
            resid_block, own_block, (((0,), (0,)), ((), ())), preferred_element_type=jnp.float32
        )
        fields = fields + shifted(early_term, "cable", -(offset + 1))
    kernel = lax.psum(kernel_part, "cable") * kernel_scale
    adjoint = (inv_norm * source_weight[None, :] * fields).reshape(2, row_count, col_count)
    return (adjoint, kernel)


def solution(mesh):
    in_specs = (
        P(None, "cable", "grid"),
        P("grid"),
        P(None, None, "cable", None),
        P(None, "cable", None),
        P("cable", None),
    )
    out_specs = (P(None, "cable", "grid"), P("grid"))
    return jax.shard_map(shards, mesh=mesh, in_specs=in_specs, out_specs=out_specs, check_vma=False)
```

profile of v0, /device:TPU:1, one launch (start us, length us, event | category | flops | bytes accessed | tf_op | source)
XLA Modules:
  0.0 386.9 jit_solution(2514229055779088914)
XLA Ops:
  7.2 0.0 all-reduce.2.cloned.1.call-start
  7.2 0.0 copy-start
  7.2 0.0 copy-start.6
  7.2 3.1 collective-permute-start
  10.3 1.6 collective-permute-start.1
  12.0 43.5 %collective-permute-done = bf16[512,2048]{1,0:T(8,128)(2,1)S(1)} collective-permute-done((bf16[512,2048]{1,0:T(8,128)(2,1)}, bf16[512,2048]{1,0:T(8,128)(2,1)S(1)}, u32[]{:S(2)}, u32[]{:S(2)}) %collective-permute-start) | collective-permute-done | bytes 2097184 | tf_op jit(solution)/shard_map/ppermute | solution.py:11
  55.4 0.0 copy-start.1
  55.4 3.6 fusion.5
  59.1 0.0 copy-done.1
  59.1 0.1 fusion.10
  59.2 24.1 %collective-permute-done.1 = bf16[512,2048]{1,0:T(8,128)(2,1)S(1)} collective-permute-done((bf16[512,2048]{1,0:T(8,128)(2,1)}, bf16[512,2048]{1,0:T(8,128)(2,1)S(1)}, u32[]{:S(2)}, u32[]{:S(2)}) %collective-permute-start.1) | collective-permute-done | bytes 2097184 | tf_op jit(solution)/shard_map/ppermute | solution.py:11
  83.3 0.0 copy-done
  83.3 0.0 copy-done.6
  83.3 0.0 copy-start.3
  83.3 1.3 fusion.3
  84.6 0.0 copy-done.3
  84.6 0.1 fusion.8
  84.7 0.1 maximum_bitcast_fusion
  84.8 0.0 copy-start.7
  84.8 0.0 copy-start.5
  84.8 1.1 pad_maximum_fusion
  85.9 0.0 all-reduce.2.cloned.1.call-update
  85.9 0.0 copy-done.7
  85.9 0.1 copy-done.5
  86.0 0.1 broadcast_multiply_fusion
  86.1 88.0 %all-reduce.2.cloned.1.call-done = f32[2,2,256,256]{3,2,1,0:T(8,128)} async-done(((f32[2,2,256,256]{3,2,1,0:T(8,128)}), f32[2,2,256,256]{3,2,1,0:T(8,128)}) %all-reduce.2.cloned.1.call-update) | async-done | bytes 1048592 | tf_op jit(solution)/shard_map/psum | solution.py:52
  174.1 1.7 multiply_convert_fusion
  175.9 1.3 fusion.13
  177.2 5.8 %collective-permute-start.2 = (f32[512,2048]{1,0:T(8,128)S(1)}, f32[512,2048]{1,0:T(8,128)S(1)}, u32[]{:S(2)}, u32[]{:S(2)}) collective-permute-start(f32[512,2048]{1,0:T(8,128)S(1)} %fusion.13), channel_id=1, source_target_pairs={{8,0},{16,8},{24,16},{32,24},{40,32},{48,40},{56,48},{64,56},{72,6... | collective-permute-start | bytes 12582920 | tf_op jit(solution)/shard_map/ppermute | solution.py:11
  182.9 0.0 copy-start.2
  182.9 1.3 fusion.11
  184.2 3.1 collective-permute-start.3
  187.4 0.0 copy-done.2
  187.4 0.0 copy-start.4
  187.4 1.3 fusion.14
  188.6 85.2 %collective-permute-done.2 = f32[512,2048]{1,0:T(8,128)S(1)} collective-permute-done((f32[512,2048]{1,0:T(8,128)S(1)}, f32[512,2048]{1,0:T(8,128)S(1)}, u32[]{:S(2)}, u32[]{:S(2)}) %collective-permute-start.2) | collective-permute-done | bytes 4194336 | tf_op jit(solution)/shard_map/ppermute | solution.py:11
  273.8 3.9 %collective-permute-done.3 = f32[512,2048]{1,0:T(8,128)S(1)} collective-permute-done((f32[512,2048]{1,0:T(8,128)S(1)}, f32[512,2048]{1,0:T(8,128)S(1)}, u32[]{:S(2)}, u32[]{:S(2)}) %collective-permute-start.3) | collective-permute-done | bytes 4194336 | tf_op jit(solution)/shard_map/ppermute | solution.py:11
  277.8 0.0 copy-done.4
  277.8 5.3 %fusion.2 = (f32[2048]{0:T(1024)S(1)}, f32[2048]{0:T(1024)S(1)}, f32[512,2048]{1,0:T(8,128)}) fusion(bf16[2,256,2048]{2,1,0:T(8,128)(2,1)S(1)} %copy-done, f32[512,2048]{1,0:T(8,128)S(1)} %fusion.14, f32[512,2048]{1,0:T(8,128)S(1)} %collective-permute-done.3, f32[512,2048]{1,0:T(8,128)S(1)} %collective-permute-done.2, ...), kind=kOutput, calls=%fused_computation.5 | convolution fusion | flops 1085272064 | bytes 21389312 | tf_op jit(solution)/shard_map/dot_general | solution.py:59
  283.1 96.4 %psum.15 = f32[2048]{0:T(1024)S(1)} all-reduce(f32[2048]{0:T(1024)S(1)} %add.27), channel_id=1, replica_groups=mesh['cable'=32,'grid'=8] {'cable'}, use_global_device_ids=true, to_apply=%region_3.0 | all-reduce | flops 2048 | bytes 16384 | tf_op jit(solution)/shard_map/psum | solution.py:68
  379.5 0.6 broadcast_multiply_fusion.1
  (5 shorter events, 0.1 us)
Async XLA Ops:
  7.2 166.9 %all-reduce.2.cloned.1.call-start = ((), (), s32[]{:S(2)}) async-start(), calls=%async_computation | async-start | bytes 2097152 | tf_op jit(solution)/shard_map/psum | solution.py:52
  7.2 76.1 %copy-start = (bf16[2,256,2048]{2,1,0:T(8,128)(2,1)S(1)}, bf16[2,256,2048]{2,1,0:T(8,128)(2,1)}, u32[]{:S(2)}) copy-start(bf16[2,256,2048]{2,1,0:T(8,128)(2,1)} %param.5) | copy-start | bytes 6291460
  7.2 76.1 %copy-start.6 = (f32[2048]{0:T(1024)S(1)}, f32[2048]{0:T(1024)}, u32[]{:S(2)}) copy-start(f32[2048]{0:T(1024)} %param.6) | copy-start | bytes 24580
  7.2 48.2 %collective-permute-start = (bf16[512,2048]{1,0:T(8,128)(2,1)}, bf16[512,2048]{1,0:T(8,128)(2,1)S(1)}, u32[]{:S(2)}, u32[]{:S(2)}) collective-permute-start(bf16[512,2048]{1,0:T(8,128)(2,1)} %bitcast.36), channel_id=1, source_target_pairs={{248,0},{0,8},{8,16},{16,24},{24,32},{32,40},{40,48},{48,56},{56,6... | collective-permute-start | bytes 6291464 | tf_op jit(solution)/shard_map/ppermute | solution.py:11
  10.3 73.0 %collective-permute-start.1 = (bf16[512,2048]{1,0:T(8,128)(2,1)}, bf16[512,2048]{1,0:T(8,128)(2,1)S(1)}, u32[]{:S(2)}, u32[]{:S(2)}) collective-permute-start(bf16[512,2048]{1,0:T(8,128)(2,1)} %bitcast.37), channel_id=1, source_target_pairs={{240,0},{248,8},{0,16},{8,24},{16,32},{24,40},{32,48},{40,56},{48,... | collective-permute-start | bytes 6291464 | tf_op jit(solution)/shard_map/ppermute | solution.py:11
  55.4 3.7 copy-start.1
  83.3 1.3 copy-start.3
  84.8 1.1 copy-start.7
  84.8 1.2 copy-start.5
  177.2 96.7 %collective-permute-start.2 = (f32[512,2048]{1,0:T(8,128)S(1)}, f32[512,2048]{1,0:T(8,128)S(1)}, u32[]{:S(2)}, u32[]{:S(2)}) collective-permute-start(f32[512,2048]{1,0:T(8,128)S(1)} %fusion.13), channel_id=1, source_target_pairs={{8,0},{16,8},{24,16},{32,24},{40,32},{48,40},{56,48},{64,56},{72,6... | collective-permute-start | bytes 12582920 | tf_op jit(solution)/shard_map/ppermute | solution.py:11
  182.9 4.4 %copy-start.2 = (bf16[512,2048]{1,0:T(8,128)(2,1)S(1)}, bf16[512,2048]{1,0:T(8,128)(2,1)}, u32[]{:S(2)}) copy-start(bf16[512,2048]{1,0:T(8,128)(2,1)} %copy-done.1) | copy-start | bytes 6291460
  184.2 93.5 %collective-permute-start.3 = (f32[512,2048]{1,0:T(8,128)S(1)}, f32[512,2048]{1,0:T(8,128)S(1)}, u32[]{:S(2)}, u32[]{:S(2)}) collective-permute-start(f32[512,2048]{1,0:T(8,128)S(1)} %fusion.11), channel_id=1, source_target_pairs={{16,0},{24,8},{32,16},{40,24},{48,32},{56,40},{64,48},{72,56},{80,... | collective-permute-start | bytes 12582920 | tf_op jit(solution)/shard_map/ppermute | solution.py:11
  187.4 90.4 %copy-start.4 = (bf16[512,2048]{1,0:T(8,128)(2,1)S(1)}, bf16[512,2048]{1,0:T(8,128)(2,1)}, u32[]{:S(2)}) copy-start(bf16[512,2048]{1,0:T(8,128)(2,1)} %copy-done.3) | copy-start | bytes 6291460
Sparse Core Ops, SparseCore 0:
  86.0 88.0 all-reduce.1
where the time goes:
time: 387 us
  waiting for transfers between devices  245 us (63%)
  blocking collectives  96.4 us (25%)
  between operations  14.2 us (4%)
  matrix products  14.1 us (4%)
  starting transfers between devices  13.7 us (4%)
    ppermute x4, waiting for transfers between devices, shifted(): return lax.ppermute(block, axis, route)  157 us
    psum x1, blocking collectives, shards(): kernel = lax.psum(kernel_part, 'cable') * kernel_scale  96.4 us
    psum x1, waiting for transfers between devices, shards(): summed = lax.psum(partials, 'grid')  88 us
    ppermute x4, starting transfers between devices, shifted(): return lax.ppermute(block, axis, route)  13.6 us
  transfers between devices with their start and end apart: 5, of which 5 were waited for; matrix products, arithmetic and copies ran while one was open for 2% of the time, Pallas kernels for 0%

commit v1 on v0

--- a/solution.py
+++ b/solution.py
@@ -3,6 +3,11 @@
 import jax.numpy as jnp
 from jax import lax
 from jax.sharding import PartitionSpec as P
+
+
+def add_all(x, mesh_axis):
+    parts = lax.all_gather(x, mesh_axis)
+    return jnp.sum(parts, axis=0)
 
 
 def shifted(block, axis, distance):
@@ -65,7 +70,7 @@
             resid_block, own_block, (((0,), (0,)), ((), ())), preferred_element_type=jnp.float32
         )
         fields = fields + shifted(early_term, "cable", -(offset + 1))
-    kernel = lax.psum(kernel_part, "cable") * kernel_scale
+    kernel = add_all(kernel_part, "cable") * kernel_scale
     adjoint = (inv_norm * source_weight[None, :] * fields).reshape(2, row_count, col_count)
     return (adjoint, kernel)
 

time: 387 us -> 367 us (0.948)
  blocking collectives: 96.4 us -> 76.5 us
    psum x1 -> x0, blocking collectives: 96.4 us -> none  [shards(): kernel = lax.psum(kernel_part, 'cable') * kernel_scale]
    all_gather x0 -> x1, blocking collectives: none -> 76.5 us  [add_all(): parts = lax.all_gather(x, mesh_axis)]
where the time goes in v1:
time: 367 us
  waiting for transfers between devices  245 us (67%)
  blocking collectives  76.5 us (21%)
  between operations  14.2 us (4%)
  matrix products  14.1 us (4%)
  starting transfers between devices  13.7 us (4%)
  other arithmetic  3.76 us (1%)
    ppermute x4, waiting for transfers between devices, shifted(): return lax.ppermute(block, axis, route)  157 us
    psum x1, waiting for transfers between devices, shards(): summed = lax.psum(partials, 'grid')  88 us
    all_gather x1, blocking collectives, add_all(): parts = lax.all_gather(x, mesh_axis)  76.5 us
    ppermute x4, starting transfers between devices, shifted(): return lax.ppermute(block, axis, route)  13.6 us
  transfers between devices with their start and end apart: 5, of which 5 were waited for; matrix products, arithmetic and copies ran while one was open for 2% of the time, Pallas kernels for 0%

profile of v1, /device:TPU:1, one launch (start us, length us, event | category | flops | bytes accessed | tf_op | source)
XLA Modules:
  0.0 367.1 jit_solution(15575863965295634467)
XLA Ops:
  7.2 0.0 all-reduce.2.cloned.1.call-start
  7.2 0.0 copy-start
  7.2 0.0 copy-start.6
  7.2 3.1 collective-permute-start
  10.3 1.6 collective-permute-start.1
  12.0 43.5 %collective-permute-done = bf16[512,2048]{1,0:T(8,128)(2,1)S(1)} collective-permute-done((bf16[512,2048]{1,0:T(8,128)(2,1)}, bf16[512,2048]{1,0:T(8,128)(2,1)S(1)}, u32[]{:S(2)}, u32[]{:S(2)}) %collective-permute-start) | collective-permute-done | bytes 2097184 | tf_op jit(solution)/shard_map/ppermute | solution.py:16
  55.4 0.0 copy-start.1
  55.4 3.6 fusion.5
  59.1 0.0 copy-done.1
  59.1 0.1 fusion.10
  59.2 24.1 %collective-permute-done.1 = bf16[512,2048]{1,0:T(8,128)(2,1)S(1)} collective-permute-done((bf16[512,2048]{1,0:T(8,128)(2,1)}, bf16[512,2048]{1,0:T(8,128)(2,1)S(1)}, u32[]{:S(2)}, u32[]{:S(2)}) %collective-permute-start.1) | collective-permute-done | bytes 2097184 | tf_op jit(solution)/shard_map/ppermute | solution.py:16
  83.3 0.0 copy-done
  83.3 0.0 copy-done.6
  83.3 0.0 copy-start.3
  83.3 1.3 fusion.3
  84.6 0.0 copy-done.3
  84.6 0.1 fusion.8
  84.7 0.1 maximum_bitcast_fusion
  84.8 0.0 copy-start.7
  84.8 0.0 copy-start.5
  84.8 1.1 pad_maximum_fusion
  85.9 0.0 all-reduce.2.cloned.1.call-update
  85.9 0.0 copy-done.7
  85.9 0.1 copy-done.5
  86.0 0.1 broadcast_multiply_fusion
  86.1 88.0 %all-reduce.2.cloned.1.call-done = f32[2,2,256,256]{3,2,1,0:T(8,128)} async-done(((f32[2,2,256,256]{3,2,1,0:T(8,128)}), f32[2,2,256,256]{3,2,1,0:T(8,128)}) %all-reduce.2.cloned.1.call-update) | async-done | bytes 1048592 | tf_op jit(solution)/shard_map/psum | solution.py:57
  174.1 1.7 multiply_convert_fusion
  175.9 1.3 fusion.13
  177.2 5.8 %collective-permute-start.2 = (f32[512,2048]{1,0:T(8,128)S(1)}, f32[512,2048]{1,0:T(8,128)S(1)}, u32[]{:S(2)}, u32[]{:S(2)}) collective-permute-start(f32[512,2048]{1,0:T(8,128)S(1)} %fusion.13), channel_id=1, source_target_pairs={{8,0},{16,8},{24,16},{32,24},{40,32},{48,40},{56,48},{64,56},{72,6... | collective-permute-start | bytes 12582920 | tf_op jit(solution)/shard_map/ppermute | solution.py:16
  182.9 0.0 copy-start.2
  182.9 1.3 fusion.11
  184.2 3.1 collective-permute-start.3
  187.4 0.0 copy-done.2
  187.4 0.0 copy-start.4
  187.4 1.3 fusion.14
  188.6 85.2 %collective-permute-done.2 = f32[512,2048]{1,0:T(8,128)S(1)} collective-permute-done((f32[512,2048]{1,0:T(8,128)S(1)}, f32[512,2048]{1,0:T(8,128)S(1)}, u32[]{:S(2)}, u32[]{:S(2)}) %collective-permute-start.2) | collective-permute-done | bytes 4194336 | tf_op jit(solution)/shard_map/ppermute | solution.py:16
  273.8 3.9 %collective-permute-done.3 = f32[512,2048]{1,0:T(8,128)S(1)} collective-permute-done((f32[512,2048]{1,0:T(8,128)S(1)}, f32[512,2048]{1,0:T(8,128)S(1)}, u32[]{:S(2)}, u32[]{:S(2)}) %collective-permute-start.3) | collective-permute-done | bytes 4194336 | tf_op jit(solution)/shard_map/ppermute | solution.py:16
  277.8 0.0 copy-done.4
  277.8 5.3 %fusion.2 = (f32[2048]{0:T(1024)S(1)}, f32[2048]{0:T(1024)S(1)}, f32[512,2048]{1,0:T(8,128)}) fusion(bf16[2,256,2048]{2,1,0:T(8,128)(2,1)S(1)} %copy-done, f32[512,2048]{1,0:T(8,128)S(1)} %fusion.14, f32[512,2048]{1,0:T(8,128)S(1)} %collective-permute-done.3, f32[512,2048]{1,0:T(8,128)S(1)} %collective-permute-done.2, ...), kind=kOutput, calls=%fused_computation.5 | convolution fusion | flops 1085272064 | bytes 21389312 | tf_op jit(solution)/shard_map/dot_general | solution.py:64
  283.1 76.5 %all-gather = f32[65536]{0:T(1024)S(1)} all-gather(f32[2048]{0:T(1024)S(1)} %add.35), channel_id=2, replica_groups=mesh['cable'=32,'grid'=8] {'cable'}, dimensions={0}, use_global_device_ids=true | all-gather | bytes 270336 | tf_op jit(solution)/shard_map/all_gather | solution.py:9
  359.7 0.6 broadcast_multiply_fusion.1
  (7 shorter events, 0.1 us)
Async XLA Ops:
  7.2 166.9 %all-reduce.2.cloned.1.call-start = ((), (), s32[]{:S(2)}) async-start(), calls=%async_computation | async-start | bytes 2097152 | tf_op jit(solution)/shard_map/psum | solution.py:57
  7.2 76.1 %copy-start = (bf16[2,256,2048]{2,1,0:T(8,128)(2,1)S(1)}, bf16[2,256,2048]{2,1,0:T(8,128)(2,1)}, u32[]{:S(2)}) copy-start(bf16[2,256,2048]{2,1,0:T(8,128)(2,1)} %param.5) | copy-start | bytes 6291460
  7.2 76.1 %copy-start.6 = (f32[2048]{0:T(1024)S(1)}, f32[2048]{0:T(1024)}, u32[]{:S(2)}) copy-start(f32[2048]{0:T(1024)} %param.6) | copy-start | bytes 24580
  7.2 48.2 %collective-permute-start = (bf16[512,2048]{1,0:T(8,128)(2,1)}, bf16[512,2048]{1,0:T(8,128)(2,1)S(1)}, u32[]{:S(2)}, u32[]{:S(2)}) collective-permute-start(bf16[512,2048]{1,0:T(8,128)(2,1)} %bitcast.36), channel_id=1, source_target_pairs={{248,0},{0,8},{8,16},{16,24},{24,32},{32,40},{40,48},{48,56},{56,6... | collective-permute-start | bytes 6291464 | tf_op jit(solution)/shard_map/ppermute | solution.py:16
  10.3 73.0 %collective-permute-start.1 = (bf16[512,2048]{1,0:T(8,128)(2,1)}, bf16[512,2048]{1,0:T(8,128)(2,1)S(1)}, u32[]{:S(2)}, u32[]{:S(2)}) collective-permute-start(bf16[512,2048]{1,0:T(8,128)(2,1)} %bitcast.37), channel_id=1, source_target_pairs={{240,0},{248,8},{0,16},{8,24},{16,32},{24,40},{32,48},{40,56},{48,... | collective-permute-start | bytes 6291464 | tf_op jit(solution)/shard_map/ppermute | solution.py:16
  55.4 3.7 copy-start.1
  83.3 1.3 copy-start.3
  84.8 1.1 copy-start.7
  84.8 1.2 copy-start.5
  177.2 96.7 %collective-permute-start.2 = (f32[512,2048]{1,0:T(8,128)S(1)}, f32[512,2048]{1,0:T(8,128)S(1)}, u32[]{:S(2)}, u32[]{:S(2)}) collective-permute-start(f32[512,2048]{1,0:T(8,128)S(1)} %fusion.13), channel_id=1, source_target_pairs={{8,0},{16,8},{24,16},{32,24},{40,32},{48,40},{56,48},{64,56},{72,6... | collective-permute-start | bytes 12582920 | tf_op jit(solution)/shard_map/ppermute | solution.py:16
  182.9 4.4 %copy-start.2 = (bf16[512,2048]{1,0:T(8,128)(2,1)S(1)}, bf16[512,2048]{1,0:T(8,128)(2,1)}, u32[]{:S(2)}) copy-start(bf16[512,2048]{1,0:T(8,128)(2,1)} %copy-done.1) | copy-start | bytes 6291460
  184.2 93.5 %collective-permute-start.3 = (f32[512,2048]{1,0:T(8,128)S(1)}, f32[512,2048]{1,0:T(8,128)S(1)}, u32[]{:S(2)}, u32[]{:S(2)}) collective-permute-start(f32[512,2048]{1,0:T(8,128)S(1)} %fusion.11), channel_id=1, source_target_pairs={{16,0},{24,8},{32,16},{40,24},{48,32},{56,40},{64,48},{72,56},{80,... | collective-permute-start | bytes 12582920 | tf_op jit(solution)/shard_map/ppermute | solution.py:16
  187.4 90.4 %copy-start.4 = (bf16[512,2048]{1,0:T(8,128)(2,1)S(1)}, bf16[512,2048]{1,0:T(8,128)(2,1)}, u32[]{:S(2)}) copy-start(bf16[512,2048]{1,0:T(8,128)(2,1)} %copy-done.3) | copy-start | bytes 6291460
Sparse Core Ops, SparseCore 0:
  86.0 88.0 all-reduce.1
